TPU v7x, 32 devices: a whole 2x2x4 slice. The times are simulated.
32 devices in a mesh: groups: 2 (over y), gx: 16 (over z, x, core).
Axes of the slice: x: 2, y: 2, z: 4, core: 2. Of those that a mesh axis runs over, the one named last changes fastest.
Arguments:
- populations: float32 [19, 32, 64, 128], P(None, ('groups', 'gx')), parts along dimension 1, may hold values from -6 to 6
- cotangent: float32 [19, 32, 64, 128], P(None, ('groups', 'gx')), parts along dimension 1, may hold values from -6 to 6
- solid_mask: int32 [32, 64, 128], P(('groups', 'gx')), parts along dimension 0, may hold values 0 or 1
- weight_in: float32 [19, 64], replicated, may hold values from -1.25 to 1.25
- weight_mid: float32 [64, 64], replicated, may hold values from -0.75 to 0.75
- weight_out: float32 [64, 19], replicated, may hold values from -0.75 to 0.75
Outputs:
- grad_populations: float32 [19, 32, 64, 128], P(None, ('groups', 'gx')), parts along dimension 1
- grad_weight_in: float32 [38, 64], P('groups'), parts along dimension 0
- grad_weight_mid: float32 [128, 64], P('groups'), parts along dimension 0
- grad_weight_out: float32 [128, 19], P('groups'), parts along dimension 0
There are 2 independent parts, one for each index of `groups`. A program takes and returns all parts, laid end to end along the dimension named above; an argument that names none is the same for every part. Nothing has to cross between parts.
Inputs may be any that keep to these rules, and one draw needn't show every extreme that they name: `solid_mask`: 1 marks a solid voxel and 0 a fluid one.
All inputs are finite; a program needn't handle non-finite values. No bound on the sum of `solid_mask` on one device may be relied on, other than what follows from the above.
Results may differ from a plain program's by a relative error of at most 0.000071.
Values sent between devices are 32-bit elements; how exact they have to be, the bound alone decides.
A program may use at most 64 MiB of HBM per device.

v0:
```python
import functools

import jax
import jax.numpy as jnp
from jax import lax
from jax.experimental import pallas as pl
from jax.experimental.pallas import tpu as pltpu
from jax.sharding import PartitionSpec as P

offset_second = (0, 1, -1, 0, 0, 0, 1, -1, 0, 0, 0, 1, -1, 0, 0, 1, 1, -1, -1)
offset_third = (0, 0, 0, 1, -1, 0, 0, 0, 1, -1, 0, 0, 0, 1, -1, 1, -1, 1, -1)
reverse_index = (5, 7, 6, 9, 8, 0, 2, 1, 4, 3, 10, 12, 11, 14, 13, 18, 17, 16, 15)

Q = 19
QP = 24
KQ = 80
ROWS = 8

f32 = jnp.float32
bf16 = jnp.bfloat16


def shifted(plane, by_y, by_z):
    if by_y:
        plane = pltpu.roll(plane, by_y % plane.shape[0], 0)
    if by_z:
        plane = pltpu.roll(plane, by_z % plane.shape[1], 1)
    return plane


def split(x):
    high = x.astype(bf16)
    return high, (x - high.astype(f32)).astype(bf16)


def dot(a, b):
    return lax.dot_general(a, b, (((1,), (0,)), ((), ())), preferred_element_type=f32)


def dot_nt(a, b):
    return lax.dot_general(a, b, (((1,), (1,)), ((), ())), preferred_element_type=f32)


def kernel(
    n, share, factor,
    pop, cot, sol, w_in, w_mid, w_out,
    out_pop, out_in, out_mid, out_out,
    X, C, S0, U, M, G, GM, S, sol_l, sol_r,
    col_l, col_r, cot_l, cot_r, gm_l, gm_r,
    H1a, H2a, D1a, D2a, Xa, H1b, H2b, D1b, D2b, Xb, GP2, GP1, Gs,
    A1, A2, A3, B1, B2, B3, tb, acc, rs, ag,
    in_sem, out_sem, sol_send, sol_recv, cot_send, cot_recv,
    col_send, col_recv, gm_send, gm_recv, rs_send, rs_recv, ag_send, ag_recv,
):
    ny, nz = X.shape[1], X.shape[2]
    hid = w_mid.shape[0]
    steps = ny // ROWS
    T = ROWS * nz
    me = lax.axis_index("gx")
    has_left, has_right = me > 0, me < n - 1
    left, right = jnp.maximum(me - 1, 0), jnp.minimum(me + 1, n - 1)

    barrier = pltpu.get_barrier_semaphore()
    for d in range(1, n):
        pl.semaphore_signal(
            barrier, inc=1, device_id={"gx": lax.rem(me + d, n)},
            device_id_type=pl.DeviceIdType.MESH,
        )

    in_x = pltpu.make_async_copy(pop, X.at[0:Q], in_sem.at[0])
    in_s = pltpu.make_async_copy(sol, S0, in_sem.at[1])
    in_c = pltpu.make_async_copy(cot, C, in_sem.at[2])
    in_x.start()
    in_s.start()
    in_c.start()

    def remote(src, dst, send, recv, device):
        return pltpu.make_async_remote_copy(
            src_ref=src, dst_ref=dst, send_sem=send, recv_sem=recv,
            device_id={"gx": device}, device_id_type=pl.DeviceIdType.MESH,
        )

    def sol_to_right():
        return remote(sol, sol_l, sol_send.at[0], sol_recv.at[0], right)

    def sol_to_left():
        return remote(sol, sol_r, sol_send.at[1], sol_recv.at[1], left)

    def cot_to_right():
        return remote(cot.at[5:10], cot_l, cot_send.at[0], cot_recv.at[0], right)

    def cot_to_left():
        return remote(cot.at[0:5], cot_r, cot_send.at[1], cot_recv.at[1], left)

    def rows_at(k):
        return pl.ds(pl.multiple_of(k * ROWS, ROWS), ROWS)

    def col_to_right(k):
        return remote(U.at[0:5, rows_at(k)], col_l.at[:, rows_at(k)], col_send.at[0, k], col_recv.at[0, k], right)

    def col_to_left(k):
        return remote(U.at[5:10, rows_at(k)], col_r.at[:, rows_at(k)], col_send.at[1, k], col_recv.at[1, k], left)

    def gm_to_right(k):
        return remote(GM.at[5:10, rows_at(k)], gm_l.at[:, rows_at(k)], gm_send.at[0, k], gm_recv.at[0, k], right)

    def gm_to_left(k):
        return remote(GM.at[0:5, rows_at(k)], gm_r.at[:, rows_at(k)], gm_send.at[1, k], gm_recv.at[1, k], left)

    def stack3(rows, period, out):
        k, m = rows.shape
        high = rows.astype(bf16).astype(f32)
        low = rows - high
        tb[...] = jnp.zeros_like(tb)
        tb[0:k, 0:m] = high
        tb[period : period + k, 0:m] = high
        tb[2 * period : 2 * period + k, 0:m] = low
        out[...] = tb[...].T[0 : out.shape[0], 0 : out.shape[1]].astype(bf16)

    def transposed(rows, keep):
        k, m = rows.shape
        tb[...] = jnp.zeros_like(tb)
        tb[0:k, 0:m] = rows
        return tb[...].T[0:keep, 0:128]

    stack3(w_in[...], QP, A1)
    stack3(w_mid[...], hid, A2)
    stack3(w_out[...], hid, A3)
    stack3(transposed(w_in[...], hid), hid, B1)
    stack3(transposed(w_mid[...], hid), hid, B2)
    stack3(transposed(w_out[...], QP), QP, B3)

    pad = jnp.zeros((QP - Q, ny, nz), f32)
    X[Q:QP] = pad
    M[Q:QP] = pad
    G[Q:QP] = pad

    @pl.when(me == 0)
    def _():
        sol_l[...] = jnp.ones_like(sol_l)
        for ref in (col_l, cot_l, gm_l):
            ref[...] = jnp.zeros_like(ref)

    @pl.when(me == n - 1)
    def _():
        sol_r[...] = jnp.ones_like(sol_r)
        for ref in (col_r, cot_r, gm_r):
            ref[...] = jnp.zeros_like(ref)

    def gather(ref, k):
        flat = ref.reshape(QP * ny, nz)
        return jnp.concatenate(
            [flat[pl.ds(k * ROWS + r, QP, stride=ny), :] for r in range(ROWS)], axis=1
        )

    def scatter(ref, k, values):
        flat = ref.reshape(QP * ny, nz)
        for r in range(ROWS):
            flat[pl.ds(k * ROWS + r, QP, stride=ny), :] = values[:, r * nz : (r + 1) * nz]

    def lanes(k):
        return pl.ds(pl.multiple_of(k * T, T), T)

    def split_q(x):
        high = x.astype(bf16).astype(f32)
        return jnp.concatenate([high, x - high, high, jnp.zeros((KQ - 3 * QP, T), f32)], axis=0).astype(bf16)

    def layer(k, stacked, weights, H, D):
        h = jnp.tanh(dot(weights[...], stacked))
        high, low = split(h)
        H[0:hid, lanes(k)] = high
        H[hid : 2 * hid, lanes(k)] = low
        D[:, lanes(k)] = 1.0 - h * h
        return jnp.concatenate([high, low, high], axis=0)

    def forward(k, src, H1, H2, D1, D2, Xs):
        x = gather(src, k)
        x3 = split_q(x)
        Xs[:, lanes(k)] = x3[0 : 2 * QP]
        h13 = layer(k, x3, A1, H1, D1)
        return x, layer(k, h13, A2, H2, D2)

    def backward(k, D1, D2):
        g = gather(G, k)
        g3 = split_q(g)
        Gs[:, lanes(k)] = g3[0 : 2 * QP]
        high, low = split(dot(B3[...], g3) * D2[:, lanes(k)])
        GP2[0:hid, lanes(k)] = high
        GP2[hid : 2 * hid, lanes(k)] = low
        p3 = jnp.concatenate([high, low, high], axis=0)
        high, low = split(dot(B2[...], p3) * D1[:, lanes(k)])
        GP1[0:hid, lanes(k)] = high
        GP1[hid : 2 * hid, lanes(k)] = low
        p3 = jnp.concatenate([high, low, high], axis=0)
        scatter(GM, k, g + dot(B1[...], p3))

    def weight_grads(H1, H2, Xs, start):
        def body(k, carry):
            m, i, o = carry
            m = m + dot_nt(H1[:, lanes(k)], GP2[:, lanes(k)])
            i = i + dot_nt(Xs[:, lanes(k)], GP1[:, lanes(k)])
            o = o + dot_nt(Gs[:, lanes(k)], H2[:, lanes(k)])
            return m, i, o

        return lax.fori_loop(0, steps, body, start)

    def propagate_back(g, from_left, from_right):
        own = S0[...] == 0
        for i in range(Q):
            o = reverse_index[i]
            if i < 5:
                src = from_right[i]
            elif i < 10:
                src = from_left[i - 5]
            else:
                src = g[i]
            moved = shifted(src, -offset_second[i], -offset_third[i])
            if i == 10:
                G[i] = g[i]
            else:
                G[i] = jnp.where(own, moved, 0.0) + jnp.where(S[o] == 0, 0.0, g[o])

    pl.semaphore_wait(barrier, n - 1)

    @pl.when(has_right)
    def _():
        sol_to_right().start()

    @pl.when(has_left)
    def _():
        sol_to_left().start()

    in_x.wait()

    def first(k, _):
        x, h23 = forward(k, X, H1a, H2a, D1a, D2a, Xa)
        scatter(U, k, x + dot(A3[...], h23))

        @pl.when(has_right)
        def _():
            col_to_right(k).start()

        @pl.when(has_left)
        def _():
            col_to_left(k).start()

        return 0

    lax.fori_loop(0, steps, first, 0)

    @pl.when(has_right)
    def _():
        cot_to_right().start()

    @pl.when(has_left)
    def _():
        cot_to_left().start()

    in_s.wait()

    @pl.when(has_left)
    def _():
        sol_to_right().wait_recv()

    @pl.when(has_right)
    def _():
        sol_to_left().wait_recv()

    for i in range(Q):
        plane = sol_l if i < 5 else sol_r if i < 10 else S0
        S[i] = shifted(plane[...], offset_second[i], offset_third[i])

    @pl.when(has_left)
    def _():
        for k in range(steps):
            col_to_right(k).wait_recv()

    @pl.when(has_right)
    def _():
        for k in range(steps):
            col_to_left(k).wait_recv()

    for i in range(Q):
        if i == 10:
            M[i] = U[i]
            continue
        src = col_l[i] if i < 5 else col_r[i - 5] if i < 10 else U[i]
        moved = shifted(src, offset_second[i], offset_third[i])
        M[i] = jnp.where(S[i] == 0, moved, U[reverse_index[i]])

    def second(k, _):
        forward(k, M, H1b, H2b, D1b, D2b, Xb)
        return 0

    lax.fori_loop(0, steps, second, 0)

    in_c.wait()

    @pl.when(has_left)
    def _():
        cot_to_right().wait_recv()

    @pl.when(has_right)
    def _():
        cot_to_left().wait_recv()

    propagate_back(C, cot_l, cot_r)

    def third(k, _):
        backward(k, D1b, D2b)

        @pl.when(has_right)
        def _():
            gm_to_right(k).start()

        @pl.when(has_left)
        def _():
            gm_to_left(k).start()

        return 0

    lax.fori_loop(0, steps, third, 0)

    zero = (jnp.zeros((2 * hid, 2 * hid), f32), jnp.zeros((2 * QP, 2 * hid), f32), jnp.zeros((2 * QP, 2 * hid), f32))
    sums = weight_grads(H1b, H2b, Xb, zero)

    @pl.when(has_left)
    def _():
        for k in range(steps):
            gm_to_right(k).wait_recv()

    @pl.when(has_right)
    def _():
        for k in range(steps):
            gm_to_left(k).wait_recv()

    propagate_back(GM, gm_l, gm_r)

    @pl.when(has_right)
    def _():
        for k in range(steps):
            gm_to_right(k).wait_send()

    @pl.when(has_left)
    def _():
        for k in range(steps):
            gm_to_left(k).wait_send()

    def fourth(k, _):
        backward(k, D1a, D2a)
        return 0

    lax.fori_loop(0, steps, fourth, 0)
    out_x = pltpu.make_async_copy(GM.at[0:Q], out_pop, out_sem.at[0])
    out_x.start()

    sum_mid, sum_in, sum_out = weight_grads(H1a, H2a, Xa, sums)

    def folded(x):
        half = x.shape[0] // 2
        x = x[0:half] + x[half:]
        return x + pltpu.roll(x, hid, 1)

    pieces = []
    for whole in (folded(sum_mid), folded(sum_in), folded(sum_out)):
        pieces += [whole[j : j + 8] for j in range(0, whole.shape[0], 8)]
    per = share // 8
    for j in range(n * per):
        piece = pieces[j] if j < len(pieces) else jnp.zeros((8, 128), f32)
        acc[j // per, (j % per) * 8 : (j % per) * 8 + 8] = piece

    def rs_copy(d):
        to = lax.rem(me + d, n)
        return remote(acc.at[to], rs.at[me], rs_send.at[d], rs_recv.at[me], to)

    def rs_arrival(d):
        source = lax.rem(me + n - d, n)
        return remote(acc.at[me], rs.at[source], rs_send.at[d], rs_recv.at[source], source)

    for d in range(1, n):
        rs_copy(d).start()
    total = acc[me]
    for d in range(1, n):
        rs_arrival(d).wait_recv()
        total = total + rs[lax.rem(me + n - d, n)]
    ag[me] = total * factor

    def ag_copy(d):
        to = lax.rem(me + d, n)
        return remote(ag.at[me], ag.at[me], ag_send.at[d], ag_recv.at[me], to)

    def ag_arrival(d):
        source = lax.rem(me + n - d, n)
        return remote(ag.at[me], ag.at[source], ag_send.at[d], ag_recv.at[source], source)

    for d in range(1, n):
        ag_copy(d).start()
    for d in range(1, n):
        ag_arrival(d).wait_recv()

    result = [ag[j // per, (j % per) * 8 : (j % per) * 8 + 8] for j in range(len(pieces))]
    count = hid // 8
    out_mid[...] = jnp.concatenate(result[0:count], axis=0)[:, 0:hid]
    out_in[...] = jnp.concatenate(result[count : count + 3], axis=0)[0:Q, 0:hid]
    last = jnp.concatenate(result[count + 3 :], axis=0)
    out_out[...] = transposed(last, 128)[0:hid, 0:Q]

    for d in range(1, n):
        rs_copy(d).wait_send()
        ag_copy(d).wait_send()

    @pl.when(has_right)
    def _():
        sol_to_right().wait_send()
        cot_to_right().wait_send()
        for k in range(steps):
            col_to_right(k).wait_send()

    @pl.when(has_left)
    def _():
        sol_to_left().wait_send()
        cot_to_left().wait_send()
        for k in range(steps):
            col_to_left(k).wait_send()

    out_x.wait()


def per_device(n, populations, cotangent, solid_mask, weight_in, weight_mid, weight_out):
    q, nx, ny, nz = populations.shape
    hid = weight_mid.shape[0]
    voxels = ny * nz
    steps = ny // ROWS
    groups_of_8 = hid // 8 + 2 * (QP // 8)
    share = 8 * -(-groups_of_8 // n)
    factor = float(nx * voxels * n) ** (-0.5)
    plane = pltpu.VMEM((ny, nz), jnp.int32)
    planes = pltpu.VMEM((QP, ny, nz), f32)
    five = pltpu.VMEM((5, ny, nz), f32)
    stack = pltpu.VMEM((2 * hid, voxels), bf16)
    slope = pltpu.VMEM((hid, voxels), f32)
    thin = pltpu.VMEM((2 * QP, voxels), bf16)
    shares = pltpu.VMEM((n, share, 128), f32)
    dma = pltpu.SemaphoreType.DMA
    grad, g_in, g_mid, g_out = pl.pallas_call(
        functools.partial(kernel, n, share, factor),
        out_shape=(
            jax.ShapeDtypeStruct((q, ny, nz), f32),
            jax.ShapeDtypeStruct(weight_in.shape, f32),
            jax.ShapeDtypeStruct(weight_mid.shape, f32),
            jax.ShapeDtypeStruct(weight_out.shape, f32),
        ),
        in_specs=[pl.BlockSpec(memory_space=pl.ANY)] * 3 + [pl.BlockSpec(memory_space=pltpu.VMEM)] * 3,
        out_specs=(pl.BlockSpec(memory_space=pl.ANY),) + (pl.BlockSpec(memory_space=pltpu.VMEM),) * 3,
        scratch_shapes=[
            planes, pltpu.VMEM((Q, ny, nz), f32), plane, planes, planes, planes, planes,
            pltpu.VMEM((Q, ny, nz), jnp.int32), plane, plane,
            five, five, five, five, five, five,
            stack, stack, slope, slope, thin,
            stack, stack, slope, slope, thin,
            stack, stack, thin,
            pltpu.VMEM((hid, KQ), bf16), pltpu.VMEM((hid, 3 * hid), bf16), pltpu.VMEM((QP, 3 * hid), bf16),
            pltpu.VMEM((QP, 3 * hid), bf16), pltpu.VMEM((hid, 3 * hid), bf16), pltpu.VMEM((hid, KQ), bf16),
            pltpu.VMEM((256, 128), f32), shares, shares, shares,
            dma((3,)), dma((1,)), dma((2,)), dma((2,)), dma((2,)), dma((2,)),
            dma((2, steps)), dma((2, steps)), dma((2, steps)), dma((2, steps)),
            dma((n,)), dma((n,)), dma((n,)), dma((n,)),
        ],
        compiler_params=pltpu.CompilerParams(
            collective_id=0, has_side_effects=True, vmem_limit_bytes=60 * 1024 * 1024
        ),
        name="lattice_backward",
    )(
        populations.reshape(q, ny, nz), cotangent.reshape(q, ny, nz), solid_mask.reshape(ny, nz),
        weight_in, weight_mid, weight_out,
    )
    return grad.reshape(populations.shape), g_in, g_mid, g_out


def solution(mesh):
    in_specs = (
        P(None, ("groups", "gx"), None, None),
        P(None, ("groups", "gx"), None, None),
        P(("groups", "gx"), None, None),
        P(),
        P(),
        P(),
    )
    out_specs = (
        P(None, ("groups", "gx"), None, None),
        P("groups", None),
        P("groups", None),
        P("groups", None),
    )
    return jax.shard_map(
        functools.partial(per_device, mesh.shape["gx"]),
        mesh=mesh, in_specs=in_specs, out_specs=out_specs, check_vma=False,
    )
```

profile of v0, /device:TPU:0, one launch (start us, length us, event | category | flops | bytes accessed | tf_op | source)
XLA Modules:
  0.0 49.7 jit_solution(2754252972522757200)
XLA Ops:
  0.6 1.4 %copy.10.w_out = f32[64,19]{1,0:T(8,128)} copy(f32[64,19]{0,1:T(8,128)} %param.11) | data formatting | bytes 9728 | tf_op args[5]
  2.0 43.0 %lattice_backward.1 = (f32[19,64,128]{2,1,0:T(8,128)}, f32[19,64]{1,0:T(8,128)}, f32[64,64]{1,0:T(8,128)}, f32[64,19]{1,0:T(8,128)}) custom-call(f32[19,64,128]{2,1,0:T(8,128)} %bitcast.6, f32[19,64,128]{2,1,0:T(8,128)} %bitcast.7, s32[64,128]{1,0:T(8,128)} %bitcast.9, f32[19,64]{1,0:T(8,128)} %w_in.1, f32[64,64]{1,0:T(8,128)} %w_mid.1, f32[64,19]{1,0:T(8,128)} %copy.10.w_out), custom_call_target="tpu_custom_call" | custom-call | tf_op jit(solution)/shard_map/lattice_backward/pallas_call | solution.py:445
  45.1 1.4 %copy.12 = f32[64,19]{0,1:T(8,128)} copy(f32[64,19]{1,0:T(8,128)} %get-tuple-element.15) | data formatting | bytes 9728
  46.5 0.0 copy-start.1
  46.5 0.0 copy-start
  46.5 2.0 %copy.16 = f32[19,1,64,128]{3,2,1,0:T(8,128)} copy(f32[19,1,64,128]{3,2,1,0:T(8,128)} %bitcast.8) | data formatting | bytes 1245184
  48.5 0.0 copy-done.1
  48.5 0.6 %copy.17 = f32[19,64]{1,0:T(8,128)} copy(f32[19,64]{1,0:T(8,128)S(1)} %copy-done.1) | data formatting | bytes 9728
  49.1 0.0 copy-done
  49.1 0.6 %copy.18 = f32[64,64]{1,0:T(8,128)} copy(f32[64,64]{1,0:T(8,128)S(1)} %copy-done) | data formatting | bytes 32768
Async XLA Ops:
  46.5 2.0 %copy-start.1 = (f32[19,64]{1,0:T(8,128)S(1)}, f32[19,64]{1,0:T(8,128)}, u32[]{:S(2)}) copy-start(f32[19,64]{1,0:T(8,128)} %get-tuple-element.21) | copy-start | bytes 14596
  46.5 2.6 %copy-start = (f32[64,64]{1,0:T(8,128)S(1)}, f32[64,64]{1,0:T(8,128)}, u32[]{:S(2)}) copy-start(f32[64,64]{1,0:T(8,128)} %get-tuple-element.22) | copy-start | bytes 49156
where the time goes:
time: 50 us; the launch traced here: 49.7 us
  Pallas kernels  43 us (86%)
  local copies, waits for them, and re-layouts  6.04 us (12%)
  between operations  0.64 us (1%)
    pallas_call x1, Pallas kernels, per_device(): pl.pallas_call(functools.partial(kernel, n, share, factor), out_shape=(ja...  43 us
    unnamed x9, local copies, waits for them, and re-layouts  6.04 us

commit v1 on v0

--- a/solution.py
+++ b/solution.py
@@ -14,7 +14,8 @@
 Q = 19
 QP = 24
 KQ = 80
-ROWS = 8
+ROWS = 32
+GAP = 8
 
 f32 = jnp.float32
 bf16 = jnp.bfloat16
@@ -43,16 +44,17 @@
 
 def kernel(
     n, share, factor,
-    pop, cot, sol, w_in, w_mid, w_out,
+    pop, cot, sol, hbm_in, hbm_mid, hbm_out,
     out_pop, out_in, out_mid, out_out,
-    X, C, S0, U, M, G, GM, S, sol_l, sol_r,
+    w_in, w_mid, w_out, X, C, S0, U, M, G, GM, S, sol_l, sol_r,
     col_l, col_r, cot_l, cot_r, gm_l, gm_r,
     H1a, H2a, D1a, D2a, Xa, H1b, H2b, D1b, D2b, Xb, GP2, GP1, Gs,
     A1, A2, A3, B1, B2, B3, tb, acc, rs, ag,
     in_sem, out_sem, sol_send, sol_recv, cot_send, cot_recv,
     col_send, col_recv, gm_send, gm_recv, rs_send, rs_recv, ag_send, ag_recv,
 ):
-    ny, nz = X.shape[1], X.shape[2]
+    ny, nz = C.shape[1], C.shape[2]
+    pitch = X.shape[1]
     hid = w_mid.shape[0]
     steps = ny // ROWS
     T = ROWS * nz
@@ -67,7 +69,13 @@
             device_id_type=pl.DeviceIdType.MESH,
         )
 
-    in_x = pltpu.make_async_copy(pop, X.at[0:Q], in_sem.at[0])
+    w_copies = [
+        pltpu.make_async_copy(a, b, in_sem.at[3 + j])
+        for j, (a, b) in enumerate(((hbm_in, w_in), (hbm_mid, w_mid), (hbm_out, w_out)))
+    ]
+    for copy in w_copies:
+        copy.start()
+    in_x = pltpu.make_async_copy(pop, X.at[0:Q, 0:ny], in_sem.at[0])
     in_s = pltpu.make_async_copy(sol, S0, in_sem.at[1])
     in_c = pltpu.make_async_copy(cot, C, in_sem.at[2])
     in_x.start()
@@ -107,7 +115,7 @@
     def gm_to_left(k):
         return remote(GM.at[0:5, rows_at(k)], gm_r.at[:, rows_at(k)], gm_send.at[1, k], gm_recv.at[1, k], left)
 
-    def stack3(rows, period, out):
+    def stack3(rows, period, out, tb):
         k, m = rows.shape
         high = rows.astype(bf16).astype(f32)
         low = rows - high
@@ -117,23 +125,22 @@
         tb[2 * period : 2 * period + k, 0:m] = low
         out[...] = tb[...].T[0 : out.shape[0], 0 : out.shape[1]].astype(bf16)
 
-    def transposed(rows, keep):
+    def transposed(rows, keep, tb):
         k, m = rows.shape
         tb[...] = jnp.zeros_like(tb)
         tb[0:k, 0:m] = rows
         return tb[...].T[0:keep, 0:128]
 
-    stack3(w_in[...], QP, A1)
-    stack3(w_mid[...], hid, A2)
-    stack3(w_out[...], hid, A3)
-    stack3(transposed(w_in[...], hid), hid, B1)
-    stack3(transposed(w_mid[...], hid), hid, B2)
-    stack3(transposed(w_out[...], QP), QP, B3)
+    for copy in w_copies:
+        copy.wait()
+    stack3(w_in[...], QP, A1, tb.at[0])
+    stack3(w_mid[...], hid, A2, tb.at[1])
+    stack3(transposed(w_out[...], hid, tb.at[2]), hid, A3, tb.at[3])
 
     pad = jnp.zeros((QP - Q, ny, nz), f32)
-    X[Q:QP] = pad
-    M[Q:QP] = pad
-    G[Q:QP] = pad
+    X[Q:QP, 0:ny] = pad
+    M[Q:QP, 0:ny] = pad
+    G[Q:QP, 0:ny] = pad
 
     @pl.when(me == 0)
     def _():
@@ -148,15 +155,15 @@
             ref[...] = jnp.zeros_like(ref)
 
     def gather(ref, k):
-        flat = ref.reshape(QP * ny, nz)
+        flat = ref.reshape(QP * pitch, nz)
         return jnp.concatenate(
-            [flat[pl.ds(k * ROWS + r, QP, stride=ny), :] for r in range(ROWS)], axis=1
+            [flat[pl.ds(k * ROWS + r, QP, stride=pitch), :] for r in range(ROWS)], axis=1
         )
 
     def scatter(ref, k, values):
-        flat = ref.reshape(QP * ny, nz)
+        flat = ref.reshape(QP * pitch, nz)
         for r in range(ROWS):
-            flat[pl.ds(k * ROWS + r, QP, stride=ny), :] = values[:, r * nz : (r + 1) * nz]
+            flat[pl.ds(k * ROWS + r, QP, stride=pitch), :] = values[:, r * nz : (r + 1) * nz]
 
     def lanes(k):
         return pl.ds(pl.multiple_of(k * T, T), T)
@@ -192,7 +199,7 @@
         GP1[0:hid, lanes(k)] = high
         GP1[hid : 2 * hid, lanes(k)] = low
         p3 = jnp.concatenate([high, low, high], axis=0)
-        scatter(GM, k, g + dot(B1[...], p3))
+        return g, p3
 
     def weight_grads(H1, H2, Xs, start):
         def body(k, carry):
@@ -213,12 +220,12 @@
             elif i < 10:
                 src = from_left[i - 5]
             else:
-                src = g[i]
+                src = g[i, 0:ny]
             moved = shifted(src, -offset_second[i], -offset_third[i])
             if i == 10:
-                G[i] = g[i]
+                G[i, 0:ny] = g[i, 0:ny]
             else:
-                G[i] = jnp.where(own, moved, 0.0) + jnp.where(S[o] == 0, 0.0, g[o])
+                G[i, 0:ny] = jnp.where(own, moved, 0.0) + jnp.where(S[o] == 0, 0.0, g[o, 0:ny])
 
     pl.semaphore_wait(barrier, n - 1)
 
@@ -256,6 +263,10 @@
     def _():
         cot_to_left().start()
 
+    stack3(transposed(w_in[...], hid, tb.at[4]), hid, B1, tb.at[5])
+    stack3(transposed(w_mid[...], hid, tb.at[6]), hid, B2, tb.at[7])
+    stack3(w_out[...], QP, B3, tb.at[8])
+
     in_s.wait()
 
     @pl.when(has_left)
@@ -282,11 +293,11 @@
 
     for i in range(Q):
         if i == 10:
-            M[i] = U[i]
+            M[i, 0:ny] = U[i, 0:ny]
             continue
-        src = col_l[i] if i < 5 else col_r[i - 5] if i < 10 else U[i]
+        src = col_l[i] if i < 5 else col_r[i - 5] if i < 10 else U[i, 0:ny]
         moved = shifted(src, offset_second[i], offset_third[i])
-        M[i] = jnp.where(S[i] == 0, moved, U[reverse_index[i]])
+        M[i, 0:ny] = jnp.where(S[i] == 0, moved, U[reverse_index[i], 0:ny])
 
     def second(k, _):
         forward(k, M, H1b, H2b, D1b, D2b, Xb)
@@ -307,7 +318,8 @@
     propagate_back(C, cot_l, cot_r)
 
     def third(k, _):
-        backward(k, D1b, D2b)
+        g, p3 = backward(k, D1b, D2b)
+        scatter(GM, k, g + dot(B1[...], p3))
 
         @pl.when(has_right)
         def _():
@@ -351,8 +363,6 @@
         return 0
 
     lax.fori_loop(0, steps, fourth, 0)
-    out_x = pltpu.make_async_copy(GM.at[0:Q], out_pop, out_sem.at[0])
-    out_x.start()
 
     sum_mid, sum_in, sum_out = weight_grads(H1a, H2a, Xa, sums)
 
@@ -379,6 +389,16 @@
 
     for d in range(1, n):
         rs_copy(d).start()
+
+    def fifth(k, _):
+        rows = GP1[:, lanes(k)]
+        scatter(GM, k, gather(G, k) + dot(B1[...], jnp.concatenate([rows, rows[0:hid]], axis=0)))
+        return 0
+
+    lax.fori_loop(0, steps, fifth, 0)
+    out_x = pltpu.make_async_copy(GM.at[0:Q, 0:ny], out_pop, out_sem.at[0])
+    out_x.start()
+
     total = acc[me]
     for d in range(1, n):
         rs_arrival(d).wait_recv()
@@ -403,7 +423,7 @@
     out_mid[...] = jnp.concatenate(result[0:count], axis=0)[:, 0:hid]
     out_in[...] = jnp.concatenate(result[count : count + 3], axis=0)[0:Q, 0:hid]
     last = jnp.concatenate(result[count + 3 :], axis=0)
-    out_out[...] = transposed(last, 128)[0:hid, 0:Q]
+    out_out[...] = last[0:Q, 0:hid]
 
     for d in range(1, n):
         rs_copy(d).wait_send()
@@ -435,7 +455,7 @@
     share = 8 * -(-groups_of_8 // n)
     factor = float(nx * voxels * n) ** (-0.5)
     plane = pltpu.VMEM((ny, nz), jnp.int32)
-    planes = pltpu.VMEM((QP, ny, nz), f32)
+    planes = pltpu.VMEM((QP, ny + GAP, nz), f32)
     five = pltpu.VMEM((5, ny, nz), f32)
     stack = pltpu.VMEM((2 * hid, voxels), bf16)
     slope = pltpu.VMEM((hid, voxels), f32)
@@ -448,11 +468,12 @@
             jax.ShapeDtypeStruct((q, ny, nz), f32),
             jax.ShapeDtypeStruct(weight_in.shape, f32),
             jax.ShapeDtypeStruct(weight_mid.shape, f32),
-            jax.ShapeDtypeStruct(weight_out.shape, f32),
+            jax.ShapeDtypeStruct((q, hid), f32),
         ),
-        in_specs=[pl.BlockSpec(memory_space=pl.ANY)] * 3 + [pl.BlockSpec(memory_space=pltpu.VMEM)] * 3,
+        in_specs=[pl.BlockSpec(memory_space=pl.ANY)] * 6,
         out_specs=(pl.BlockSpec(memory_space=pl.ANY),) + (pl.BlockSpec(memory_space=pltpu.VMEM),) * 3,
         scratch_shapes=[
+            pltpu.VMEM((q, hid), f32), pltpu.VMEM((hid, hid), f32), pltpu.VMEM((q, hid), f32),
             planes, pltpu.VMEM((Q, ny, nz), f32), plane, planes, planes, planes, planes,
             pltpu.VMEM((Q, ny, nz), jnp.int32), plane, plane,
             five, five, five, five, five, five,
@@ -461,8 +482,8 @@
             stack, stack, thin,
             pltpu.VMEM((hid, KQ), bf16), pltpu.VMEM((hid, 3 * hid), bf16), pltpu.VMEM((QP, 3 * hid), bf16),
             pltpu.VMEM((QP, 3 * hid), bf16), pltpu.VMEM((hid, 3 * hid), bf16), pltpu.VMEM((hid, KQ), bf16),
-            pltpu.VMEM((256, 128), f32), shares, shares, shares,
-            dma((3,)), dma((1,)), dma((2,)), dma((2,)), dma((2,)), dma((2,)),
+            pltpu.VMEM((9, 256, 128), f32), shares, shares, shares,
+            dma((6,)), dma((1,)), dma((2,)), dma((2,)), dma((2,)), dma((2,)),
             dma((2, steps)), dma((2, steps)), dma((2, steps)), dma((2, steps)),
             dma((n,)), dma((n,)), dma((n,)), dma((n,)),
         ],
@@ -472,9 +493,9 @@
         name="lattice_backward",
     )(
         populations.reshape(q, ny, nz), cotangent.reshape(q, ny, nz), solid_mask.reshape(ny, nz),
-        weight_in, weight_mid, weight_out,
+        weight_in, weight_mid, weight_out.T,
     )
-    return grad.reshape(populations.shape), g_in, g_mid, g_out
+    return grad.reshape(populations.shape), g_in, g_mid, g_out.T
 
 
 def solution(mesh):

time: 50 us -> 39.7 us (0.79)
  Pallas kernels: 43 us -> 34.9 us
  local copies, waits for them, and re-layouts: 6.04 us -> 3.89 us
    pallas_call x1, Pallas kernels: 43 us -> 34.9 us  [per_device(): pl.pallas_call(functools.partial(kernel, n, share, factor), out_shape=(ja...]
    unnamed x9 -> x10, local copies, waits for them, and re-layouts: 6.04 us -> 3.89 us
where the time goes in v1:
time: 39.7 us; the launch traced here: 39.4 us
  Pallas kernels  34.9 us (88%)
  local copies, waits for them, and re-layouts  3.89 us (10%)
  between operations  0.66 us (2%)
    pallas_call x1, Pallas kernels, per_device(): pl.pallas_call(functools.partial(kernel, n, share, factor), out_shape=(ja...  34.9 us
    unnamed x10, local copies, waits for them, and re-layouts  3.89 us

profile of v1, /device:TPU:0, one launch (start us, length us, event | category | flops | bytes accessed | tf_op | source)
XLA Modules:
  0.0 39.4 jit_solution(16582607254499013470)
XLA Ops:
  0.6 34.9 %lattice_backward.1 = (f32[19,64,128]{2,1,0:T(8,128)}, f32[19,64]{1,0:T(8,128)}, f32[64,64]{1,0:T(8,128)}, f32[19,64]{1,0:T(8,128)}) custom-call(f32[19,64,128]{2,1,0:T(8,128)} %bitcast.8, f32[19,64,128]{2,1,0:T(8,128)} %bitcast.9, s32[64,128]{1,0:T(8,128)} %bitcast.11, f32[19,64]{1,0:T(8,128)} %hbm_in.1, f32[64,64]{1,0:T(8,128)} %hbm_mid.1, f32[19,64]{1,0:T(8,128)} %bitcast.13), custom_call_target="tpu_custom_call" | custom-call | tf_op jit(solution)/shard_map/lattice_backward/pallas_call | solution.py:465
  35.5 0.0 copy-start.2
  35.5 0.0 copy-start
  35.5 2.0 %copy.15 = f32[19,1,64,128]{3,2,1,0:T(8,128)} copy(f32[19,1,64,128]{3,2,1,0:T(8,128)} %bitcast.10) | data formatting | bytes 1245184
  37.5 0.0 copy-done.2
  37.5 0.6 %copy.16 = f32[19,64]{1,0:T(8,128)} copy(f32[19,64]{1,0:T(8,128)S(1)} %copy-done.2) | data formatting | bytes 9728
  38.1 0.0 copy-done
  38.1 0.0 copy-start.1
  38.1 0.6 %copy.17 = f32[64,64]{1,0:T(8,128)} copy(f32[64,64]{1,0:T(8,128)S(1)} %copy-done) | data formatting | bytes 32768
  38.7 0.1 copy-done.1
  38.8 0.6 %copy.18 = f32[64,19]{0,1:T(8,128)} copy(f32[64,19]{0,1:T(8,128)S(1)} %bitcast.12) | data formatting | bytes 9728
Async XLA Ops:
  35.5 2.0 %copy-start.2 = (f32[19,64]{1,0:T(8,128)S(1)}, f32[19,64]{1,0:T(8,128)}, u32[]{:S(2)}) copy-start(f32[19,64]{1,0:T(8,128)} %get-tuple-element.21) | copy-start | bytes 14596
  35.5 2.6 %copy-start = (f32[64,64]{1,0:T(8,128)S(1)}, f32[64,64]{1,0:T(8,128)}, u32[]{:S(2)}) copy-start(f32[64,64]{1,0:T(8,128)} %get-tuple-element.22) | copy-start | bytes 49156
  38.1 0.7 %copy-start.1 = (f32[19,64]{1,0:T(8,128)S(1)}, f32[19,64]{1,0:T(8,128)}, u32[]{:S(2)}) copy-start(f32[19,64]{1,0:T(8,128)} %get-tuple-element.11) | copy-start | bytes 14596

commit v2 on v1

--- a/solution.py
+++ b/solution.py
@@ -1,4 +1,5 @@
 import functools
+import math
 
 import jax
 import jax.numpy as jnp
@@ -49,9 +50,9 @@
     w_in, w_mid, w_out, X, C, S0, U, M, G, GM, S, sol_l, sol_r,
     col_l, col_r, cot_l, cot_r, gm_l, gm_r,
     H1a, H2a, D1a, D2a, Xa, H1b, H2b, D1b, D2b, Xb, GP2, GP1, Gs,
-    A1, A2, A3, B1, B2, B3, tb, acc, rs, ag,
+    A1, A2, A3, B1, B2, B3, tb, acc, rs, across, ag,
     in_sem, out_sem, sol_send, sol_recv, cot_send, cot_recv,
-    col_send, col_recv, gm_send, gm_recv, rs_send, rs_recv, ag_send, ag_recv,
+    col_send, col_recv, gm_send, gm_recv, rs_send, rs_recv, ac_send, ac_recv, ag_send, ag_recv,
 ):
     ny, nz = C.shape[1], C.shape[2]
     pitch = X.shape[1]
@@ -227,21 +228,22 @@
             else:
                 G[i, 0:ny] = jnp.where(own, moved, 0.0) + jnp.where(S[o] == 0, 0.0, g[o, 0:ny])
 
-    pl.semaphore_wait(barrier, n - 1)
-
-    @pl.when(has_right)
-    def _():
-        sol_to_right().start()
-
-    @pl.when(has_left)
-    def _():
-        sol_to_left().start()
-
     in_x.wait()
 
-    def first(k, _):
+    def first(k):
         x, h23 = forward(k, X, H1a, H2a, D1a, D2a, Xa)
         scatter(U, k, x + dot(A3[...], h23))
+
+        if k == 0:
+            pl.semaphore_wait(barrier, n - 1)
+
+            @pl.when(has_right)
+            def _():
+                sol_to_right().start()
+
+            @pl.when(has_left)
+            def _():
+                sol_to_left().start()
 
         @pl.when(has_right)
         def _():
@@ -251,9 +253,8 @@
         def _():
             col_to_left(k).start()
 
-        return 0
-
-    lax.fori_loop(0, steps, first, 0)
+    for k in range(steps):
+        first(k)
 
     @pl.when(has_right)
     def _():
@@ -375,19 +376,24 @@
     for whole in (folded(sum_mid), folded(sum_in), folded(sum_out)):
         pieces += [whole[j : j + 8] for j in range(0, whole.shape[0], 8)]
     per = share // 8
-    for j in range(n * per):
+    for j in range(acc.shape[0] * per):
         piece = pieces[j] if j < len(pieces) else jnp.zeros((8, 128), f32)
         acc[j // per, (j % per) * 8 : (j % per) * 8 + 8] = piece
 
+    inner = acc.shape[0]
+    outer = n // inner
+    mine, group = lax.rem(me, inner), me // inner
+    first_of_group = group * inner
+
     def rs_copy(d):
-        to = lax.rem(me + d, n)
-        return remote(acc.at[to], rs.at[me], rs_send.at[d], rs_recv.at[me], to)
+        to = lax.rem(mine + d, inner)
+        return remote(acc.at[to], rs.at[mine], rs_send.at[d], rs_recv.at[mine], first_of_group + to)
 
     def rs_arrival(d):
-        source = lax.rem(me + n - d, n)
-        return remote(acc.at[me], rs.at[source], rs_send.at[d], rs_recv.at[source], source)
-
-    for d in range(1, n):
+        source = lax.rem(mine + inner - d, inner)
+        return remote(acc.at[mine], rs.at[source], rs_send.at[d], rs_recv.at[source], first_of_group + source)
+
+    for d in range(1, inner):
         rs_copy(d).start()
 
     def fifth(k, _):
@@ -399,23 +405,40 @@
     out_x = pltpu.make_async_copy(GM.at[0:Q, 0:ny], out_pop, out_sem.at[0])
     out_x.start()
 
-    total = acc[me]
-    for d in range(1, n):
+    total = acc[mine]
+    for d in range(1, inner):
         rs_arrival(d).wait_recv()
-        total = total + rs[lax.rem(me + n - d, n)]
-    ag[me] = total * factor
+        total = total + rs[lax.rem(mine + inner - d, inner)]
+    across[group] = total
+
+    def ac_copy(d):
+        to = lax.rem(group + d, outer) * inner + mine
+        return remote(across.at[group], across.at[group], ac_send.at[d], ac_recv.at[group], to)
+
+    def ac_arrival(d):
+        source = lax.rem(group + outer - d, outer)
+        return remote(across.at[group], across.at[source], ac_send.at[d], ac_recv.at[source], source * inner + mine)
+
+    for d in range(1, outer):
+        ac_copy(d).start()
+    for d in range(1, outer):
+        ac_arrival(d).wait_recv()
+    total = across[0]
+    for j in range(1, outer):
+        total = total + across[j]
+    ag[mine] = total * factor
 
     def ag_copy(d):
-        to = lax.rem(me + d, n)
-        return remote(ag.at[me], ag.at[me], ag_send.at[d], ag_recv.at[me], to)
+        to = first_of_group + lax.rem(mine + d, inner)
+        return remote(ag.at[mine], ag.at[mine], ag_send.at[d], ag_recv.at[mine], to)
 
     def ag_arrival(d):
-        source = lax.rem(me + n - d, n)
-        return remote(ag.at[me], ag.at[source], ag_send.at[d], ag_recv.at[source], source)
-
-    for d in range(1, n):
+        source = lax.rem(mine + inner - d, inner)
+        return remote(ag.at[mine], ag.at[source], ag_send.at[d], ag_recv.at[source], first_of_group + source)
+
+    for d in range(1, inner):
         ag_copy(d).start()
-    for d in range(1, n):
+    for d in range(1, inner):
         ag_arrival(d).wait_recv()
 
     result = [ag[j // per, (j % per) * 8 : (j % per) * 8 + 8] for j in range(len(pieces))]
@@ -425,9 +448,11 @@
     last = jnp.concatenate(result[count + 3 :], axis=0)
     out_out[...] = last[0:Q, 0:hid]
 
-    for d in range(1, n):
+    for d in range(1, inner):
         rs_copy(d).wait_send()
         ag_copy(d).wait_send()
+    for d in range(1, outer):
+        ac_copy(d).wait_send()
 
     @pl.when(has_right)
     def _():
@@ -444,6 +469,28 @@
             col_to_left(k).wait_send()
 
     out_x.wait()
+
+
+def hand_on(*refs):
+    n = (len(refs) - 2) // 3
+    sources, targets, held = refs[:n], refs[n : 2 * n], refs[2 * n : 3 * n]
+    in_sem, out_sem = refs[3 * n :]
+    parts = [(sources[j], held[j], targets[j]) for j in range(1, n)]
+    q = sources[0].shape[0]
+    for at in range(0, q, 5):
+        rows = pl.ds(at, min(5, q - at))
+        parts.append((sources[0].at[rows], held[0].at[rows], targets[0].at[rows]))
+    copies = [
+        (pltpu.make_async_copy(a, b, in_sem.at[j]), pltpu.make_async_copy(b, c, out_sem.at[j]))
+        for j, (a, b, c) in enumerate(parts)
+    ]
+    for one, _ in copies:
+        one.start()
+    for one, two in copies:
+        one.wait()
+        two.start()
+    for _, two in copies:
+        two.wait()
 
 
 def per_device(n, populations, cotangent, solid_mask, weight_in, weight_mid, weight_out):
@@ -452,7 +499,9 @@
     voxels = ny * nz
     steps = ny // ROWS
     groups_of_8 = hid // 8 + 2 * (QP // 8)
-    share = 8 * -(-groups_of_8 // n)
+    inner = math.gcd(n, 4)
+    outer = n // inner
+    share = 8 * -(-groups_of_8 // inner)
     factor = float(nx * voxels * n) ** (-0.5)
     plane = pltpu.VMEM((ny, nz), jnp.int32)
     planes = pltpu.VMEM((QP, ny + GAP, nz), f32)
@@ -460,7 +509,7 @@
     stack = pltpu.VMEM((2 * hid, voxels), bf16)
     slope = pltpu.VMEM((hid, voxels), f32)
     thin = pltpu.VMEM((2 * QP, voxels), bf16)
-    shares = pltpu.VMEM((n, share, 128), f32)
+    shares = pltpu.VMEM((inner, share, 128), f32)
     dma = pltpu.SemaphoreType.DMA
     grad, g_in, g_mid, g_out = pl.pallas_call(
         functools.partial(kernel, n, share, factor),
@@ -482,10 +531,10 @@
             stack, stack, thin,
             pltpu.VMEM((hid, KQ), bf16), pltpu.VMEM((hid, 3 * hid), bf16), pltpu.VMEM((QP, 3 * hid), bf16),
             pltpu.VMEM((QP, 3 * hid), bf16), pltpu.VMEM((hid, 3 * hid), bf16), pltpu.VMEM((hid, KQ), bf16),
-            pltpu.VMEM((9, 256, 128), f32), shares, shares, shares,
+            pltpu.VMEM((9, 256, 128), f32), shares, shares, pltpu.VMEM((outer, share, 128), f32), shares,
             dma((6,)), dma((1,)), dma((2,)), dma((2,)), dma((2,)), dma((2,)),
             dma((2, steps)), dma((2, steps)), dma((2, steps)), dma((2, steps)),
-            dma((n,)), dma((n,)), dma((n,)), dma((n,)),
+            dma((inner,)), dma((inner,)), dma((outer,)), dma((outer,)), dma((inner,)), dma((inner,)),
         ],
         compiler_params=pltpu.CompilerParams(
             collective_id=0, has_side_effects=True, vmem_limit_bytes=60 * 1024 * 1024
@@ -495,6 +544,16 @@
         populations.reshape(q, ny, nz), cotangent.reshape(q, ny, nz), solid_mask.reshape(ny, nz),
         weight_in, weight_mid, weight_out.T,
     )
+    results = (grad, g_in, g_mid, g_out)
+    copies = len(results) - 1 + -(-q // 5)
+    grad, g_in, g_mid, g_out = pl.pallas_call(
+        hand_on,
+        out_shape=tuple(jax.ShapeDtypeStruct(r.shape, r.dtype) for r in results),
+        in_specs=[pl.BlockSpec(memory_space=pl.ANY)] * 4,
+        out_specs=(pl.BlockSpec(memory_space=pl.ANY),) * 4,
+        scratch_shapes=[pltpu.VMEM(r.shape, r.dtype) for r in results] + [dma((copies,)), dma((copies,))],
+        name="hand_on",
+    )(*results)
     return grad.reshape(populations.shape), g_in, g_mid, g_out.T
 
 

time: 39.7 us -> 36.5 us (0.919)
  local copies, waits for them, and re-layouts: 3.89 us -> 0 us
  Pallas kernels: 34.9 us -> 35.5 us
    unnamed x10 -> x0, local copies, waits for them, and re-layouts: 3.89 us -> none
    pallas_call x0 -> x1, Pallas kernels: none -> 1.97 us  [per_device(): pl.pallas_call(hand_on, out_shape=tuple((jax.ShapeDtypeStruct(r.shape, r....]
    pallas_call x1, Pallas kernels: 34.9 us -> 33.5 us  [per_device(): pl.pallas_call(functools.partial(kernel, n, share, factor), out_shape=(ja...]
where the time goes in v2:
time: 36.5 us; the launch traced here: 36.2 us
  Pallas kernels  35.5 us (97%)
  between operations  0.64 us (2%)
    pallas_call x1, Pallas kernels, per_device(): pl.pallas_call(functools.partial(kernel, n, share, factor), out_shape=(ja...  33.5 us
    pallas_call x1, Pallas kernels, per_device(): pl.pallas_call(hand_on, out_shape=tuple((jax.ShapeDtypeStruct(r.shape, r....  1.97 us

profile of v2, /device:TPU:0, one launch (start us, length us, event | category | flops | bytes accessed | tf_op | source)
XLA Modules:
  0.0 36.2 jit_solution(11114783975320147840)
XLA Ops:
  0.6 33.5 %lattice_backward.1 = (f32[19,64,128]{2,1,0:T(8,128)}, f32[19,64]{1,0:T(8,128)}, f32[64,64]{1,0:T(8,128)}, f32[19,64]{1,0:T(8,128)}) custom-call(f32[19,64,128]{2,1,0:T(8,128)} %bitcast.8, f32[19,64,128]{2,1,0:T(8,128)} %bitcast.9, s32[64,128]{1,0:T(8,128)} %bitcast.10, f32[19,64]{1,0:T(8,128)} %hbm_in.1, f32[64,64]{1,0:T(8,128)} %hbm_mid.1, f32[19,64]{1,0:T(8,128)} %bitcast.11), custom_call_target="tpu_custom_call" | custom-call | tf_op jit(solution)/shard_map/lattice_backward/pallas_call | solution.py:514
  34.2 2.0 %hand_on.1 = (f32[19,64,128]{2,1,0:T(8,128)}, f32[19,64]{1,0:T(8,128)}, f32[64,64]{1,0:T(8,128)}, f32[19,64]{1,0:T(8,128)}) custom-call(f32[19,64,128]{2,1,0:T(8,128)} %get-tuple-element.12.refs_0_, f32[19,64]{1,0:T(8,128)} %get-tuple-element.13.refs_1_, f32[64,64]{1,0:T(8,128)} %get-tuple-element.14.refs_2_, f32[19,64]{1,0:T(8,128)} %get-tuple-element.15.refs_3_), custom_call_target="tpu_custom_call" | custom-call | tf_op jit(solution)/shard_map/hand_on/pallas_call | solution.py:549

commit v3 on v2

--- a/solution.py
+++ b/solution.py
@@ -304,7 +304,8 @@
         forward(k, M, H1b, H2b, D1b, D2b, Xb)
         return 0
 
-    lax.fori_loop(0, steps, second, 0)
+    for k in range(steps):
+        second(k, 0)
 
     in_c.wait()
 
@@ -332,7 +333,8 @@
 
         return 0
 
-    lax.fori_loop(0, steps, third, 0)
+    for k in range(steps):
+        third(k, 0)
 
     zero = (jnp.zeros((2 * hid, 2 * hid), f32), jnp.zeros((2 * QP, 2 * hid), f32), jnp.zeros((2 * QP, 2 * hid), f32))
     sums = weight_grads(H1b, H2b, Xb, zero)
@@ -363,7 +365,8 @@
         backward(k, D1a, D2a)
         return 0
 
-    lax.fori_loop(0, steps, fourth, 0)
+    for k in range(steps):
+        fourth(k, 0)
 
     sum_mid, sum_in, sum_out = weight_grads(H1a, H2a, Xa, sums)
 
@@ -401,7 +404,8 @@
         scatter(GM, k, gather(G, k) + dot(B1[...], jnp.concatenate([rows, rows[0:hid]], axis=0)))
         return 0
 
-    lax.fori_loop(0, steps, fifth, 0)
+    for k in range(steps):
+        fifth(k, 0)
     out_x = pltpu.make_async_copy(GM.at[0:Q, 0:ny], out_pop, out_sem.at[0])
     out_x.start()
 

time: 36.5 us -> 36.2 us (level)
  no operation moved by 1% of the time
where the time goes in v3:
time: 36.2 us; the launch traced here: 35.9 us
  Pallas kernels  35.2 us (97%)
  between operations  0.64 us (2%)
    pallas_call x1, Pallas kernels, per_device(): pl.pallas_call(functools.partial(kernel, n, share, factor), out_shape=(ja...  33.3 us
    pallas_call x1, Pallas kernels, per_device(): pl.pallas_call(hand_on, out_shape=tuple((jax.ShapeDtypeStruct(r.shape, r....  1.97 us

profile of v3, /device:TPU:0, one launch (start us, length us, event | category | flops | bytes accessed | tf_op | source)
XLA Modules:
  0.0 35.9 jit_solution(3485370131443095144)
XLA Ops:
  0.6 33.3 %lattice_backward.1 = (f32[19,64,128]{2,1,0:T(8,128)}, f32[19,64]{1,0:T(8,128)}, f32[64,64]{1,0:T(8,128)}, f32[19,64]{1,0:T(8,128)}) custom-call(f32[19,64,128]{2,1,0:T(8,128)} %bitcast.8, f32[19,64,128]{2,1,0:T(8,128)} %bitcast.9, s32[64,128]{1,0:T(8,128)} %bitcast.10, f32[19,64]{1,0:T(8,128)} %hbm_in.1, f32[64,64]{1,0:T(8,128)} %hbm_mid.1, f32[19,64]{1,0:T(8,128)} %bitcast.11), custom_call_target="tpu_custom_call" | custom-call | tf_op jit(solution)/shard_map/lattice_backward/pallas_call | solution.py:518
  33.9 2.0 %hand_on.1 = (f32[19,64,128]{2,1,0:T(8,128)}, f32[19,64]{1,0:T(8,128)}, f32[64,64]{1,0:T(8,128)}, f32[19,64]{1,0:T(8,128)}) custom-call(f32[19,64,128]{2,1,0:T(8,128)} %get-tuple-element.12.refs_0_, f32[19,64]{1,0:T(8,128)} %get-tuple-element.13.refs_1_, f32[64,64]{1,0:T(8,128)} %get-tuple-element.14.refs_2_, f32[19,64]{1,0:T(8,128)} %get-tuple-element.15.refs_3_), custom_call_target="tpu_custom_call" | custom-call | tf_op jit(solution)/shard_map/hand_on/pallas_call | solution.py:553
